TPU v7x, 32 devices: a whole 2x2x4 slice. The times are simulated.
32 devices in a mesh: slab: 4 (over y, x), box: 8 (over z, core).
Axes of the slice: x: 2, y: 2, z: 4, core: 2. Of those that a mesh axis runs over, the one named last changes fastest.
Arguments:
- sources: bfloat16 [4, 8, 512, 4096], P('slab', 'box'), may hold values from -6 to 6
- leaf_ops: bfloat16 [4, 8, 256, 4096], P('slab', 'box'), may hold values from -0.09375 to 0.09375
- edge_slot: int32 [4, 8, 256], P('slab', 'box'), may hold values from 0 to 255, each once within a row
- merge_ops: float32 [4, 8, 256, 256], P('slab', 'box'), may hold values from -0.25 to 0.25
- lift_ops: float32 [4, 8, 512, 256], P('slab', 'box'), may hold values from -0.375 to 0.375
- coupling: float32 [4, 512, 512], P('slab', 'box'), may hold values from -0.125 to 0.125
- inverse: float32 [4, 512, 512], P('slab', 'box'), may hold values from -0.25 to 0.25
- boundary: float32 [512, 512], P(None, 'box'), may hold values from -6 to 6
Outputs:
- interface_solution: float32 [4, 512, 512], P('slab', None, 'box')
Inputs may be any that keep to these rules, and one draw needn't show every extreme that they name: Each row edge_slot[s, b] holds every number from 0 to 255 once.
All inputs are finite; a program needn't handle non-finite values.
Results may differ from a plain program's by a relative error of at most 0.0003.
Values sent between devices are 32-bit elements; how exact they have to be, the bound alone decides.
A program may use at most 64 MiB of HBM per device.

v0:
```python
import jax
import jax.numpy as jnp
from jax import lax
from jax.sharding import PartitionSpec as P

highest = lax.Precision.HIGHEST
contract_last = (((1,), (1,)), ((), ()))


def partner(value, axis, bit):
    mask = 2**bit
    pairs = [(source, source ^ mask) for source in range(lax.axis_size(axis))]
    return lax.ppermute(value, axis, pairs)


def from_behind(value, axis, by):
    count = lax.axis_size(axis)
    pairs = [(i, i + by) for i in range(count) if 0 <= i + by < count]
    return lax.ppermute(value, axis, pairs)


def pass_partner(given_rows, bit_number):
    return partner(given_rows, "box", bit_number)


def hand_on(solution):
    return from_behind(solution, "slab", 1)


def advance(entering, slab_load, coupling_rows, inverse_rows):
    columns = coupling_rows
    coupled = lax.dot_general(
        lax.all_gather(entering, "box", axis=1, tiled=True),
        columns,
        contract_last,
        precision=highest,
        preferred_element_type=jnp.float32,
    )
    corrected = slab_load - coupled
    columns = inverse_rows
    return lax.dot_general(
        lax.all_gather(corrected, "box", axis=1, tiled=True),
        columns,
        contract_last,
        precision=highest,
        preferred_element_type=jnp.float32,
    )


def on_device(sources, leaf_ops, edge_slot, merge_ops, lift_ops, coupling, inverse, boundary):
    sources_box = sources[0, 0]
    leaf_box = leaf_ops[0, 0]
    slot_box = edge_slot[0, 0]
    merge_box = merge_ops[0, 0]
    lift_box = lift_ops[0, 0]
    coupling_rows = coupling[0]
    inverse_rows = inverse[0]
    box_flux = lax.dot_general(
        sources_box, leaf_box, contract_last, preferred_element_type=jnp.float32
    )
    current = jnp.take(box_flux, slot_box, axis=1)
    levels = lax.axis_size("box").bit_length() - 1
    position = lax.axis_index("box")
    for tree_level in range(levels):
        bit_number = levels - 1 - tree_level
        merged = lax.dot_general(
            current, merge_box, contract_last, precision=highest, preferred_element_type=jnp.float32
        )
        half_rows = current.shape[0] // 2
        upper_half = jnp.bitwise_and(jnp.right_shift(position, bit_number), 1)
        kept_rows = lax.dynamic_slice_in_dim(merged, upper_half * half_rows, half_rows, 0)
        given_rows = lax.dynamic_slice_in_dim(merged, (1 - upper_half) * half_rows, half_rows, 0)
        current = kept_rows + pass_partner(given_rows, bit_number)
    lifted = lax.dot_general(
        current, lift_box, contract_last, precision=highest, preferred_element_type=jnp.float32
    )
    slab_load = lax.all_to_all(lifted, "box", split_axis=1, concat_axis=0, tiled=True)
    slab_position = lax.axis_index("slab")
    n_slab = lax.axis_size("slab")
    incoming = boundary
    solution = slab_load
    for section in range(n_slab):
        entering = jnp.where(slab_position == 0, boundary, incoming)
        solution = advance(entering, slab_load, coupling_rows, inverse_rows)
        if section + 1 < n_slab:
            incoming = hand_on(solution)
    return solution[None]


def solution(mesh):
    return jax.shard_map(
        on_device,
        mesh=mesh,
        in_specs=(
            P("slab", "box", None, None),
            P("slab", "box", None, None),
            P("slab", "box", None),
            P("slab", "box", None, None),
            P("slab", "box", None, None),
            P("slab", "box", None),
            P("slab", "box", None),
            P(None, "box"),
        ),
        out_specs=P("slab", None, "box"),
        check_vma=False,
    )
```

profile of v0, /device:TPU:7, one launch (start us, length us, event | category | flops | bytes accessed | tf_op | source)
XLA Modules:
  0.0 266.0 jit_solution(3155124362095147405)
XLA Ops:
  8.7 3.5 %fusion = f32[512,256]{0,1:T(8,128)S(1)} fusion(bf16[1,1,512,4096]{3,2,1,0:T(8,128)(2,1)} %param.8, bf16[1,1,256,4096]{3,2,1,0:T(8,128)(2,1)S(1)} %copy-done), kind=kOutput, calls=%fused_computation.1 | convolution fusion | flops 1073741824 | bytes 6815744 | tf_op jit(solution)/shard_map/dot_general | solution.py:58
  14.3 2.4 collective-permute-start
  16.7 17.8 %collective-permute-done = f32[256,256]{1,0:T(8,128)} collective-permute-done((f32[256,256]{1,0:T(8,128)S(1)}, f32[256,256]{1,0:T(8,128)}, u32[]{:S(2)}, u32[]{:S(2)}) %collective-permute-start) | collective-permute-done | bytes 262176 | tf_op jit(solution)/shard_map/ppermute | solution.py:13
  35.9 3.5 %collective-permute-start.1 = (f32[128,256]{1,0:T(8,128)S(1)}, f32[128,256]{1,0:T(8,128)S(1)}, u32[]{:S(2)}, u32[]{:S(2)}) collective-permute-start(f32[128,256]{1,0:T(8,128)S(1)} %constant_dynamic-slice_fusion.1), channel_id=1, source_target_pairs={{0,2},{1,3},{2,0},{3,1},{4,6},{5,7},{6,4},{7,5},{8,10},{9,11},{10,... | collective-permute-start | bytes 393224 | tf_op jit(solution)/shard_map/ppermute | solution.py:13
  39.4 2.4 collective-permute-done.1
  42.2 2.9 %collective-permute-start.2 = (f32[64,256]{1,0:T(8,128)S(1)}, f32[64,256]{1,0:T(8,128)S(1)}, u32[]{:S(2)}, u32[]{:S(2)}) collective-permute-start(f32[64,256]{1,0:T(8,128)S(1)} %constant_dynamic-slice_fusion), channel_id=1, source_target_pairs={{0,1},{1,0},{2,3},{3,2},{4,5},{5,4},{6,7},{7,6},{8,9},{9,8},{10,11... | collective-permute-start | bytes 196616 | tf_op jit(solution)/shard_map/ppermute | solution.py:13
  48.1 11.1 %all_to_all.16 = f32[8,1,4096]{2,1,0:T(1,128)S(1)} all-to-all(f32[8,1,4096]{2,1,0:T(1,128)S(1)} %reshape.48), channel_id=1, replica_groups=mesh['slab'=4,'box'=8] {'box'}, dimensions={0} | all-to-all | bytes 262144 | tf_op jit(solution)/shard_map/all_to_all | solution.py:77
  61.0 2.7 %convolution_subtract_fusion.3 = f32[512,64]{0,1:T(8,128)} fusion(f32[512,64]{0,1:T(8,128)S(1)} %copy.13, f32[512,512]{0,1:T(8,128)} %all-gather.9.cloned.1.call-done, f32[1,64,512]{2,1,0:T(8,128)S(1)} %copy-done.4), kind=kOutput, calls=%fused_computation.8 | convolution fusion | flops 201359360 | bytes 1441792 | tf_op jit(solution)/shard_map/dot_general | solution.py:32
  63.7 22.1 %all-gather.11.cloned.1.call-done = f32[512,512]{0,1:T(8,128)} async-done(((f32[512,64]{0,1:T(8,128)}), f32[512,512]{0,1:T(8,128)}) %all-gather.11.cloned.1.call-update) | async-done | bytes 1048592 | tf_op jit(solution)/shard_map/all_gather | solution.py:42
  89.1 5.4 %collective-permute-done.3 = f32[512,64]{0,1:T(8,128)S(1)} collective-permute-done((f32[512,64]{0,1:T(8,128)S(1)}, f32[512,64]{0,1:T(8,128)S(1)}, u32[]{:S(2)}, u32[]{:S(2)}) %collective-permute-start.3) | collective-permute-done | bytes 131104 | tf_op jit(solution)/shard_map/ppermute | solution.py:19
  95.2 22.8 %all-gather.13.cloned.1.call-done = f32[512,512]{0,1:T(8,128)} async-done(((f32[512,64]{0,1:T(8,128)}), f32[512,512]{0,1:T(8,128)}) %all-gather.13.cloned.1.call-update) | async-done | bytes 1048592 | tf_op jit(solution)/shard_map/all_gather | solution.py:33
  118.0 2.7 %convolution_subtract_fusion.2 = f32[512,64]{0,1:T(8,128)} fusion(f32[512,64]{0,1:T(8,128)S(1)} %copy.13, f32[512,512]{0,1:T(8,128)} %all-gather.13.cloned.1.call-done, f32[1,64,512]{2,1,0:T(8,128)S(1)} %copy-done.4), kind=kOutput, calls=%fused_computation.7 | convolution fusion | flops 201359360 | bytes 1441792 | tf_op jit(solution)/shard_map/dot_general | solution.py:32
  120.7 22.0 %all-gather.15.cloned.1.call-done = f32[512,512]{0,1:T(8,128)} async-done(((f32[512,64]{0,1:T(8,128)}), f32[512,512]{0,1:T(8,128)}) %all-gather.15.cloned.1.call-update) | async-done | bytes 1048592 | tf_op jit(solution)/shard_map/all_gather | solution.py:42
  142.7 2.0 fusion.17
  146.0 5.4 %collective-permute-done.4 = f32[512,64]{0,1:T(8,128)S(1)} collective-permute-done((f32[512,64]{0,1:T(8,128)S(1)}, f32[512,64]{0,1:T(8,128)S(1)}, u32[]{:S(2)}, u32[]{:S(2)}) %collective-permute-start.4) | collective-permute-done | bytes 131104 | tf_op jit(solution)/shard_map/ppermute | solution.py:19
  152.1 22.8 %all-gather.17.cloned.1.call-done = f32[512,512]{0,1:T(8,128)} async-done(((f32[512,64]{0,1:T(8,128)}), f32[512,512]{0,1:T(8,128)}) %all-gather.17.cloned.1.call-update) | async-done | bytes 1048592 | tf_op jit(solution)/shard_map/all_gather | solution.py:33
  174.9 2.7 %convolution_subtract_fusion.1 = f32[512,64]{0,1:T(8,128)} fusion(f32[512,64]{0,1:T(8,128)S(1)} %copy.13, f32[512,512]{0,1:T(8,128)} %all-gather.17.cloned.1.call-done, f32[1,64,512]{2,1,0:T(8,128)S(1)} %copy-done.4), kind=kOutput, calls=%fused_computation.6 | convolution fusion | flops 201359360 | bytes 1441792 | tf_op jit(solution)/shard_map/dot_general | solution.py:32
  177.6 22.0 %all-gather.19.cloned.1.call-done = f32[512,512]{0,1:T(8,128)} async-done(((f32[512,64]{0,1:T(8,128)}), f32[512,512]{0,1:T(8,128)}) %all-gather.19.cloned.1.call-update) | async-done | bytes 1048592 | tf_op jit(solution)/shard_map/all_gather | solution.py:42
  199.6 2.0 fusion.15
  202.9 5.4 %collective-permute-done.5 = f32[512,64]{0,1:T(8,128)S(1)} collective-permute-done((f32[512,64]{0,1:T(8,128)S(1)}, f32[512,64]{0,1:T(8,128)S(1)}, u32[]{:S(2)}, u32[]{:S(2)}) %collective-permute-start.5) | collective-permute-done | bytes 131104 | tf_op jit(solution)/shard_map/ppermute | solution.py:19
  209.0 22.8 %all-gather.21.cloned.1.call-done = f32[512,512]{0,1:T(8,128)} async-done(((f32[512,64]{0,1:T(8,128)}), f32[512,512]{0,1:T(8,128)}) %all-gather.21.cloned.1.call-update) | async-done | bytes 1048592 | tf_op jit(solution)/shard_map/all_gather | solution.py:33
  231.8 2.7 %convolution_subtract_fusion = f32[512,64]{0,1:T(8,128)} fusion(f32[512,64]{0,1:T(8,128)S(1)} %copy.13, f32[512,512]{0,1:T(8,128)} %all-gather.21.cloned.1.call-done, f32[1,64,512]{2,1,0:T(8,128)S(1)} %copy-done.4), kind=kOutput, calls=%fused_computation.5 | convolution fusion | flops 201359360 | bytes 1441792 | tf_op jit(solution)/shard_map/dot_general | solution.py:32
  234.5 22.0 %all-gather.23.cloned.1.call-done = f32[512,512]{0,1:T(8,128)} async-done(((f32[512,64]{0,1:T(8,128)}), f32[512,512]{0,1:T(8,128)}) %all-gather.23.cloned.1.call-update) | async-done | bytes 1048592 | tf_op jit(solution)/shard_map/all_gather | solution.py:42
  256.5 2.7 %convolution_bitcast_fusion = f32[1,512,64]{1,2,0:T(8,128)} fusion(f32[512,512]{0,1:T(8,128)} %all-gather.23.cloned.1.call-done, f32[1,64,512]{2,1,0:T(8,128)S(1)} %copy-done.2), kind=kOutput, calls=%fused_computation.4 | convolution fusion | flops 201326592 | bytes 1310720 | tf_op jit(solution)/shard_map/dot_general | solution.py:41
  (51 shorter events, 19.0 us)
Async XLA Ops:
  6.5 2.2 copy-start
  6.5 54.4 %all-gather.9.cloned.1.call-start = ((), (), s32[]{:S(2)}) async-start(), calls=%async_computation.1 | async-start | bytes 1179648 | tf_op jit(solution)/shard_map/all_gather | solution.py:33
  7.3 78.5 %all-gather.11.cloned.1.call-start = ((), (), s32[]{:S(2)}) async-start(), calls=%async_computation.2 | async-start | bytes 1179648 | tf_op jit(solution)/shard_map/all_gather | solution.py:42
  12.2 1.0 copy-start.1
  13.2 72.6 %copy-start.2 = (f32[1,64,512]{2,1,0:T(8,128)S(1)}, f32[1,64,512]{2,1,0:T(8,128)}, u32[]{:S(2)}) copy-start(f32[1,64,512]{2,1,0:T(8,128)} %param.14) | copy-start | bytes 393220
  14.2 46.7 %copy-start.4 = (f32[1,64,512]{2,1,0:T(8,128)S(1)}, f32[1,64,512]{2,1,0:T(8,128)}, u32[]{:S(2)}) copy-start(f32[1,64,512]{2,1,0:T(8,128)} %param.13) | copy-start | bytes 393220
  14.3 80.2 %copy-start.3 = (f32[512,64]{0,1:T(8,128)S(1)}, f32[512,64]{0,1:T(8,128)}, u32[]{:S(2)}) copy-start(f32[512,64]{0,1:T(8,128)} %param.15) | copy-start | bytes 393220
  14.3 20.2 %collective-permute-start = (f32[256,256]{1,0:T(8,128)S(1)}, f32[256,256]{1,0:T(8,128)}, u32[]{:S(2)}, u32[]{:S(2)}) collective-permute-start(f32[256,256]{1,0:T(8,128)S(1)} %constant_dynamic-slice_fusion.2), channel_id=1, source_target_pairs={{0,4},{1,5},{2,6},{3,7},{4,0},{5,1},{6,2},{7,3},{8,12},{9,13},{10,... | collective-permute-start | bytes 786440 | tf_op jit(solution)/shard_map/ppermute | solution.py:13
  35.9 5.9 %collective-permute-start.1 = (f32[128,256]{1,0:T(8,128)S(1)}, f32[128,256]{1,0:T(8,128)S(1)}, u32[]{:S(2)}, u32[]{:S(2)}) collective-permute-start(f32[128,256]{1,0:T(8,128)S(1)} %constant_dynamic-slice_fusion.1), channel_id=1, source_target_pairs={{0,2},{1,3},{2,0},{3,1},{4,6},{5,7},{6,4},{7,5},{8,10},{9,11},{10,... | collective-permute-start | bytes 393224 | tf_op jit(solution)/shard_map/ppermute | solution.py:13
  42.2 3.8 %collective-permute-start.2 = (f32[64,256]{1,0:T(8,128)S(1)}, f32[64,256]{1,0:T(8,128)S(1)}, u32[]{:S(2)}, u32[]{:S(2)}) collective-permute-start(f32[64,256]{1,0:T(8,128)S(1)} %constant_dynamic-slice_fusion), channel_id=1, source_target_pairs={{0,1},{1,0},{2,3},{3,2},{4,5},{5,4},{6,7},{7,6},{8,9},{9,8},{10,11... | collective-permute-start | bytes 196616 | tf_op jit(solution)/shard_map/ppermute | solution.py:13
  63.7 54.3 %all-gather.13.cloned.1.call-start = ((), (), s32[]{:S(2)}) async-start(), calls=%async_computation.3 | async-start | bytes 1179648 | tf_op jit(solution)/shard_map/all_gather | solution.py:33
  87.8 6.7 %collective-permute-start.3 = (f32[512,64]{0,1:T(8,128)S(1)}, f32[512,64]{0,1:T(8,128)S(1)}, u32[]{:S(2)}, u32[]{:S(2)}) collective-permute-start(f32[512,64]{0,1:T(8,128)S(1)} %fusion.19), channel_id=1, source_target_pairs={{0,8},{8,16},{16,24},{1,9},{9,17},{17,25},{2,10},{10,18},{18,26},{... | collective-permute-start | bytes 393224 | tf_op jit(solution)/shard_map/ppermute | solution.py:19
  95.1 47.5 %all-gather.15.cloned.1.call-start = ((), (), s32[]{:S(2)}) async-start(), calls=%async_computation.4 | async-start | bytes 1179648 | tf_op jit(solution)/shard_map/all_gather | solution.py:42
  120.7 54.2 %all-gather.17.cloned.1.call-start = ((), (), s32[]{:S(2)}) async-start(), calls=%async_computation.5 | async-start | bytes 1179648 | tf_op jit(solution)/shard_map/all_gather | solution.py:33
  144.7 6.7 %collective-permute-start.4 = (f32[512,64]{0,1:T(8,128)S(1)}, f32[512,64]{0,1:T(8,128)S(1)}, u32[]{:S(2)}, u32[]{:S(2)}) collective-permute-start(f32[512,64]{0,1:T(8,128)S(1)} %fusion.17), channel_id=1, source_target_pairs={{0,8},{8,16},{16,24},{1,9},{9,17},{17,25},{2,10},{10,18},{18,26},{... | collective-permute-start | bytes 393224 | tf_op jit(solution)/shard_map/ppermute | solution.py:19
  152.0 47.5 %all-gather.19.cloned.1.call-start = ((), (), s32[]{:S(2)}) async-start(), calls=%async_computation.6 | async-start | bytes 1179648 | tf_op jit(solution)/shard_map/all_gather | solution.py:42
  177.6 54.2 %all-gather.21.cloned.1.call-start = ((), (), s32[]{:S(2)}) async-start(), calls=%async_computation.7 | async-start | bytes 1179648 | tf_op jit(solution)/shard_map/all_gather | solution.py:33
  201.6 6.7 %collective-permute-start.5 = (f32[512,64]{0,1:T(8,128)S(1)}, f32[512,64]{0,1:T(8,128)S(1)}, u32[]{:S(2)}, u32[]{:S(2)}) collective-permute-start(f32[512,64]{0,1:T(8,128)S(1)} %fusion.15), channel_id=1, source_target_pairs={{0,8},{8,16},{16,24},{1,9},{9,17},{17,25},{2,10},{10,18},{18,26},{... | collective-permute-start | bytes 393224 | tf_op jit(solution)/shard_map/ppermute | solution.py:19
  208.9 47.5 %all-gather.23.cloned.1.call-start = ((), (), s32[]{:S(2)}) async-start(), calls=%async_computation.8 | async-start | bytes 1179648 | tf_op jit(solution)/shard_map/all_gather | solution.py:42
Sparse Core Ops, SparseCore 0:
  8.9 29.7 all-gather.8
  63.8 21.9 all-gather.10
  95.3 22.6 all-gather.12
  120.8 21.8 all-gather.14
  152.2 22.6 all-gather.16
  177.7 21.8 all-gather.18
  209.1 22.6 all-gather.20
  234.6 21.8 all-gather.22
where the time goes:
time: 268 us; the launch traced here: 266 us
  waiting for transfers between devices  194 us (72%)
  matrix products  27.6 us (10%)
  between operations  13.7 us (5%)
  starting transfers between devices  12.9 us (5%)
  blocking collectives  11.1 us (4%)
  other arithmetic  4.35 us (2%)
    all_gather x4, waiting for transfers between devices, advance(): lax.all_gather(corrected, 'box', axis=1, tiled=True)  88 us
    all_gather x4, waiting for transfers between devices, advance(): lax.all_gather(entering, 'box', axis=1, tiled=True)  68.4 us
    ppermute x3, waiting for transfers between devices, partner(): return lax.ppermute(value, axis, pairs)  21.1 us
    ppermute x3, waiting for transfers between devices, from_behind(): return lax.ppermute(value, axis, pairs)  16.1 us
    all_to_all x1, blocking collectives, on_device(): lax.all_to_all(lifted, 'box', split_axis=1, concat_axis=0, tiled=True)  11.1 us
    dot_general x4, matrix products, advance(): lax.dot_general(lax.all_gather(entering, 'box', axis=1, tiled=True), colu...  10.7 us
    ppermute x3, starting transfers between devices, partner(): return lax.ppermute(value, axis, pairs)  8.77 us
    dot_general x4, matrix products, advance(): lax.dot_general(lax.all_gather(corrected, 'box', axis=1, tiled=True), col...  8.68 us
  transfers between devices with their start and end apart: 14, of which 13 were waited for; matrix products, arithmetic and copies ran while one was open for 5% of the time, Pallas kernels for 0%

commit v1 on v0

v1 whole, which is shorter than its diff:
```python
import jax
import jax.numpy as jnp
from jax import lax
from jax.sharding import PartitionSpec as P

high = lax.Precision.HIGH
contract_last = (((1,), (1,)), ((), ()))


def mm_t(a, b, dims=contract_last):
    return lax.dot_general(a, b, dims, precision=high, preferred_element_type=jnp.float32)


def on_device(sources, leaf_ops, edge_slot, merge_ops, lift_ops, coupling, inverse, boundary):
    slot_box = edge_slot[0, 0]
    merge_box = merge_ops[0, 0]
    lift_box = lift_ops[0, 0]
    coupling_all = lax.all_gather(coupling[0], "box", axis=0, tiled=True)
    inverse_all = lax.all_gather(inverse[0], "box", axis=0, tiled=True)
    edges = slot_box.shape[0]
    onehot = (slot_box[:, None] == lax.broadcasted_iota(jnp.int32, (edges, edges), 1)).astype(jnp.float32)
    first = mm_t(merge_box, onehot, (((1,), (0,)), ((), ())))
    entering = lax.all_to_all(boundary, "box", split_axis=0, concat_axis=1, tiled=True)
    current = lax.dot_general(
        sources[0, 0], leaf_ops[0, 0], contract_last, preferred_element_type=jnp.float32
    )
    n_box = lax.axis_size("box")
    levels = n_box.bit_length() - 1
    position = lax.axis_index("box")
    for level in range(levels):
        bit = levels - 1 - level
        merged = mm_t(current, first if level == 0 else merge_box)
        half = current.shape[0] // 2
        upper = jnp.bitwise_and(jnp.right_shift(position, bit), 1)
        kept = lax.dynamic_slice_in_dim(merged, upper * half, half, 0)
        given = lax.dynamic_slice_in_dim(merged, (1 - upper) * half, half, 0)
        pairs = [(i, i ^ (1 << bit)) for i in range(n_box)]
        current = kept + lax.ppermute(given, "box", pairs)
    load = mm_t(current, lift_box)
    own = mm_t(load, inverse_all)
    carry = mm_t(inverse_all, coupling_all, (((1,), (0,)), ((), ())))
    n_slab = lax.axis_size("slab")
    slab = lax.axis_index("slab")
    incoming = entering
    for section in range(n_slab):
        state = own - mm_t(incoming, carry)
        if section + 1 < n_slab:
            passed = lax.ppermute(state, "slab", [(i, i + 1) for i in range(n_slab - 1)])
            incoming = jnp.where(slab == 0, entering, passed)
    return lax.all_to_all(state, "box", split_axis=1, concat_axis=0, tiled=True)[None]


def solution(mesh):
    return jax.shard_map(
        on_device,
        mesh=mesh,
        in_specs=(
            P("slab", "box", None, None),
            P("slab", "box", None, None),
            P("slab", "box", None),
            P("slab", "box", None, None),
            P("slab", "box", None, None),
            P("slab", "box", None),
            P("slab", "box", None),
            P(None, "box"),
        ),
        out_specs=P("slab", None, "box"),
        check_vma=False,
    )
```

time: 268 us -> 110 us (0.41)
  the two profiles are of different devices: /device:TPU:7 before, /device:TPU:4 now
where the time goes in v1:
time: 110 us; the launch traced here: 109 us
  waiting for transfers between devices  50.4 us (46%)
  starting transfers between devices  16.5 us (15%)
  matrix products  13.8 us (13%)
  between operations  13.6 us (12%)
  blocking collectives  9.99 us (9%)
  local copies, waits for them, and re-layouts  3.22 us (3%)
  other arithmetic  1.7 us (2%)
    ppermute x3, waiting for transfers between devices, on_device(): current = kept + lax.ppermute(given, 'box', pairs)  20.4 us
    ppermute x3, waiting for transfers between devices, on_device(): lax.ppermute(state, 'slab', [(i, i + 1) for i in range(n_slab - 1)])  16.3 us
    dot_general x11, matrix products, mm_t(): lax.dot_general(a, b, dims, precision=high, preferred_element_type=jnp.fl...  10.3 us
    all_to_all x1, blocking collectives, on_device(): lax.all_to_all(state, 'box', split_axis=1, concat_axis=0, tiled=True)[None]  9.99 us
    ppermute x3, starting transfers between devices, on_device(): lax.ppermute(state, 'slab', [(i, i + 1) for i in range(n_slab - 1)])  7.82 us
    all_gather x1, waiting for transfers between devices, on_device(): coupling_all = lax.all_gather(coupling[0], 'box', axis=0, tiled=True)  6.48 us
    all_to_all x1, waiting for transfers between devices, on_device(): lax.all_to_all(boundary, 'box', split_axis=0, concat_axis=1, tiled=True)  5.84 us
    all_to_all x1, starting transfers between devices, on_device(): lax.all_to_all(boundary, 'box', split_axis=0, concat_axis=1, tiled=True)  4.66 us
  transfers between devices with their start and end apart: 9, of which 6 were waited for; matrix products, arithmetic and copies ran while one was open for 10% of the time, Pallas kernels for 0%

profile of v1, /device:TPU:4, one launch (start us, length us, event | category | flops | bytes accessed | tf_op | source)
XLA Modules:
  0.0 109.2 jit_solution(448189653500081825)
XLA Ops:
  6.5 0.7 all-gather.5.cloned.1.call-update
  7.3 0.7 all-gather.7.cloned.1.call-update
  8.1 3.5 %fusion = f32[512,256]{1,0:T(8,128)S(1)} fusion(bf16[1,1,512,4096]{3,2,1,0:T(8,128)(2,1)} %param.8, bf16[1,1,256,4096]{3,2,1,0:T(8,128)(2,1)S(1)} %copy-done), kind=kOutput, calls=%fused_computation | convolution fusion | flops 1073741824 | bytes 6815744 | tf_op jit(solution)/shard_map/dot_general | solution.py:24
  12.4 2.7 %collective-permute-start = (f32[256,256]{1,0:T(8,128)S(1)}, f32[256,256]{1,0:T(8,128)S(1)}, u32[]{:S(2)}, u32[]{:S(2)}) collective-permute-start(f32[256,256]{1,0:T(8,128)S(1)} %constant_dynamic-slice_fusion.2), channel_id=1, source_target_pairs={{0,4},{1,5},{2,6},{3,7},{4,0},{5,1},{6,2},{7,3},{8,12},{9,13},{10,... | collective-permute-start | bytes 786440 | tf_op jit(solution)/shard_map/ppermute | solution.py:38
  15.1 20.4 %collective-permute-done = f32[256,256]{1,0:T(8,128)S(1)} collective-permute-done((f32[256,256]{1,0:T(8,128)S(1)}, f32[256,256]{1,0:T(8,128)S(1)}, u32[]{:S(2)}, u32[]{:S(2)}) %collective-permute-start) | collective-permute-done | bytes 262176 | tf_op jit(solution)/shard_map/ppermute | solution.py:38
  35.9 0.7 collective-permute-start.1
  36.7 0.8 reshape.10
  37.6 4.7 %all-to-all-start = ((f32[8,1,4096]{2,1,0:T(1,128)}), f32[8,1,4096]{2,1,0:T(1,128)S(1)}, u32[]{:S(2)}, u32[]{:S(2)}) async-start(f32[8,1,4096]{2,1,0:T(1,128)} %reshape.10), calls=%async_computation | async-start | bytes 262144 | tf_op jit(solution)/shard_map/all_to_all | solution.py:23
  43.2 5.8 %all-to-all-done = f32[8,1,4096]{2,1,0:T(1,128)S(1)} async-done(((f32[8,1,4096]{2,1,0:T(1,128)}), f32[8,1,4096]{2,1,0:T(1,128)S(1)}, u32[]{:S(2)}, u32[]{:S(2)}) %all-to-all-start) | async-done | bytes 131104 | tf_op jit(solution)/shard_map/all_to_all | solution.py:23
  49.5 0.9 reduce
  50.7 1.4 %fusion.9 = f32[64,512]{1,0:T(8,128)S(1)} fusion(f32[1,1,512,256]{3,2,1,0:T(8,128)} %param.12, f32[64,256]{1,0:T(8,128)S(1)} %collective-permute-done.2, f32[128,256]{1,0:T(8,128)S(1)} %fusion.11, s32[]{:T(128)S(6)} %select_n.38), kind=kOutput, calls=%fused_computation.13 | convolution fusion | flops 50348032 | bytes 786436 | tf_op jit(solution)/shard_map/dot_general | solution.py:11
  52.2 1.8 %fusion.7 = f32[64,512]{1,0:T(8,128)S(1)} fusion(f32[64,512]{1,0:T(8,128)S(1)} %fusion.9, f32[1,512,512]{2,1,0:T(8,128)} %all-gather.5.cloned.1.call-done), kind=kOutput, calls=%fused_computation.11 | convolution fusion | flops 100663296 | bytes 1310720 | tf_op jit(solution)/shard_map/dot_general | solution.py:11
  54.0 6.5 %all-gather.7.cloned.1.call-done = f32[1,512,512]{2,1,0:T(8,128)} async-done(((f32[1,64,512]{2,1,0:T(8,128)}), f32[1,512,512]{2,1,0:T(8,128)}) %all-gather.7.cloned.1.call-update) | async-done | bytes 1048592 | tf_op jit(solution)/shard_map/all_gather | solution.py:18
  60.5 2.5 %fusion.4 = f32[512,512]{1,0:T(8,128)S(1)} fusion(f32[1,512,512]{2,1,0:T(8,128)} %all-gather.7.cloned.1.call-done, f32[1,512,512]{2,1,0:T(8,128)} %all-gather.5.cloned.1.call-done), kind=kOutput, calls=%fused_computation.8 | convolution fusion | flops 805306368 | bytes 3145728 | tf_op jit(solution)/shard_map/dot_general | solution.py:11
  63.0 1.3 %fusion.3 = f32[64,512]{1,0:T(8,128)} fusion(f32[64,512]{1,0:T(8,128)S(1)} %fusion.7, f32[512,512]{1,0:T(8,128)S(1)} %fusion.4, f32[64,512]{1,0:T(8,128)S(1)} %all_to_all.29), kind=kOutput, calls=%fused_computation.7 | convolution fusion | flops 100696064 | bytes 1441792 | tf_op jit(solution)/shard_map/dot_general | solution.py:11
  64.3 3.4 %collective-permute-start.3 = (f32[64,512]{1,0:T(8,128)}, f32[64,512]{1,0:T(8,128)S(1)}, u32[]{:S(2)}, u32[]{:S(2)}) collective-permute-start(f32[64,512]{1,0:T(8,128)} %fusion.3), channel_id=1, source_target_pairs={{0,8},{8,16},{16,24},{1,9},{9,17},{17,25},{2,10},{10,18},{18,26},{... | collective-permute-start | bytes 393224 | tf_op jit(solution)/shard_map/ppermute | solution.py:48
  67.7 5.2 %collective-permute-done.3 = f32[64,512]{1,0:T(8,128)S(1)} collective-permute-done((f32[64,512]{1,0:T(8,128)}, f32[64,512]{1,0:T(8,128)S(1)}, u32[]{:S(2)}, u32[]{:S(2)}) %collective-permute-start.3) | collective-permute-done | bytes 131104 | tf_op jit(solution)/shard_map/ppermute | solution.py:48
  73.5 2.5 %collective-permute-start.4 = (f32[64,512]{1,0:T(8,128)S(1)}, f32[64,512]{1,0:T(8,128)S(1)}, u32[]{:S(2)}, u32[]{:S(2)}) collective-permute-start(f32[64,512]{1,0:T(8,128)S(1)} %convolution_subtract_fusion.2), channel_id=1, source_target_pairs={{0,8},{8,16},{16,24},{1,9},{9,17},{17,25},{2,10},{10,18},{18,26},{... | collective-permute-start | bytes 393224 | tf_op jit(solution)/shard_map/ppermute | solution.py:48
  76.1 5.2 %collective-permute-done.4 = f32[64,512]{1,0:T(8,128)S(1)} collective-permute-done((f32[64,512]{1,0:T(8,128)S(1)}, f32[64,512]{1,0:T(8,128)S(1)}, u32[]{:S(2)}, u32[]{:S(2)}) %collective-permute-start.4) | collective-permute-done | bytes 131104 | tf_op jit(solution)/shard_map/ppermute | solution.py:48
  81.9 1.9 %collective-permute-start.5 = (f32[64,512]{1,0:T(8,128)S(1)}, f32[64,512]{1,0:T(8,128)S(1)}, u32[]{:S(2)}, u32[]{:S(2)}) collective-permute-start(f32[64,512]{1,0:T(8,128)S(1)} %convolution_subtract_fusion.1), channel_id=1, source_target_pairs={{0,8},{8,16},{16,24},{1,9},{9,17},{17,25},{2,10},{10,18},{18,26},{... | collective-permute-start | bytes 393224 | tf_op jit(solution)/shard_map/ppermute | solution.py:48
  83.8 5.8 %collective-permute-done.5 = f32[64,512]{1,0:T(8,128)S(1)} collective-permute-done((f32[64,512]{1,0:T(8,128)S(1)}, f32[64,512]{1,0:T(8,128)S(1)}, u32[]{:S(2)}, u32[]{:S(2)}) %collective-permute-start.5) | collective-permute-done | bytes 131104 | tf_op jit(solution)/shard_map/ppermute | solution.py:48
  90.6 10.0 %all_to_all.35 = f32[8,1,4096]{2,1,0:T(1,128)S(1)} all-to-all(f32[8,1,4096]{2,1,0:T(1,128)S(1)} %reshape.12), channel_id=1, replica_groups=mesh['slab'=4,'box'=8] {'box'}, dimensions={0} | all-to-all | bytes 262144 | tf_op jit(solution)/shard_map/all_to_all | solution.py:50
  100.6 0.9 reduce.1
  101.6 0.8 copy.14
  (33 shorter events, 5.4 us)
Async XLA Ops:
  6.5 1.6 %copy-start = (bf16[1,1,256,4096]{3,2,1,0:T(8,128)(2,1)S(1)}, bf16[1,1,256,4096]{3,2,1,0:T(8,128)(2,1)}, u32[]{:S(2)}) copy-start(bf16[1,1,256,4096]{3,2,1,0:T(8,128)(2,1)} %param.9) | copy-start | bytes 6291460
  6.5 5.1 %copy-start.1 = (f32[1,1,256,256]{3,2,1,0:T(8,128)S(1)}, f32[1,1,256,256]{3,2,1,0:T(8,128)}, u32[]{:S(2)}) copy-start(f32[1,1,256,256]{3,2,1,0:T(8,128)} %param.11) | copy-start | bytes 786436
  6.5 5.1 %copy-start.3 = (s32[1,1,256]{2,1,0:T(1,128)S(1)}, s32[1,1,256]{2,1,0:T(1,128)}, u32[]{:S(2)}) copy-start(s32[1,1,256]{2,1,0:T(1,128)} %param.10) | copy-start | bytes 3076
  6.5 45.6 %all-gather.5.cloned.1.call-start = ((), (), s32[]{:S(2)}) async-start(), calls=%async_computation.2 | async-start | bytes 1179648 | tf_op jit(solution)/shard_map/all_gather | solution.py:19
  7.3 53.2 %all-gather.7.cloned.1.call-start = ((), (), s32[]{:S(2)}) async-start(), calls=%async_computation.3 | async-start | bytes 1179648 | tf_op jit(solution)/shard_map/all_gather | solution.py:18
  8.1 28.5 %copy-start.2 = (f32[512,64]{0,1:T(8,128)S(1)}, f32[512,64]{0,1:T(8,128)}, u32[]{:S(2)}) copy-start(f32[512,64]{0,1:T(8,128)} %param.15) | copy-start | bytes 393220
  12.4 23.1 %collective-permute-start = (f32[256,256]{1,0:T(8,128)S(1)}, f32[256,256]{1,0:T(8,128)S(1)}, u32[]{:S(2)}, u32[]{:S(2)}) collective-permute-start(f32[256,256]{1,0:T(8,128)S(1)} %constant_dynamic-slice_fusion.2), channel_id=1, source_target_pairs={{0,4},{1,5},{2,6},{3,7},{4,0},{5,1},{6,2},{7,3},{8,12},{9,13},{10,... | collective-permute-start | bytes 786440 | tf_op jit(solution)/shard_map/ppermute | solution.py:38
  35.9 6.4 %collective-permute-start.1 = (f32[128,256]{1,0:T(8,128)S(1)}, f32[128,256]{1,0:T(8,128)S(1)}, u32[]{:S(2)}, u32[]{:S(2)}) collective-permute-start(f32[128,256]{1,0:T(8,128)S(1)} %constant_dynamic-slice_fusion.1), channel_id=1, source_target_pairs={{0,2},{1,3},{2,0},{3,1},{4,6},{5,7},{6,4},{7,5},{8,10},{9,11},{10,... | collective-permute-start | bytes 393224 | tf_op jit(solution)/shard_map/ppermute | solution.py:38
  37.6 11.4 %all-to-all-start = ((f32[8,1,4096]{2,1,0:T(1,128)}), f32[8,1,4096]{2,1,0:T(1,128)S(1)}, u32[]{:S(2)}, u32[]{:S(2)}) async-start(f32[8,1,4096]{2,1,0:T(1,128)} %reshape.10), calls=%async_computation | async-start | bytes 262144 | tf_op jit(solution)/shard_map/all_to_all | solution.py:23
  42.6 8.1 %collective-permute-start.2 = (f32[64,256]{1,0:T(8,128)S(1)}, f32[64,256]{1,0:T(8,128)S(1)}, u32[]{:S(2)}, u32[]{:S(2)}) collective-permute-start(f32[64,256]{1,0:T(8,128)S(1)} %constant_dynamic-slice_fusion), channel_id=1, source_target_pairs={{0,1},{1,0},{2,3},{3,2},{4,5},{5,4},{6,7},{7,6},{8,9},{9,8},{10,11... | collective-permute-start | bytes 196616 | tf_op jit(solution)/shard_map/ppermute | solution.py:38
  64.3 8.6 %collective-permute-start.3 = (f32[64,512]{1,0:T(8,128)}, f32[64,512]{1,0:T(8,128)S(1)}, u32[]{:S(2)}, u32[]{:S(2)}) collective-permute-start(f32[64,512]{1,0:T(8,128)} %fusion.3), channel_id=1, source_target_pairs={{0,8},{8,16},{16,24},{1,9},{9,17},{17,25},{2,10},{10,18},{18,26},{... | collective-permute-start | bytes 393224 | tf_op jit(solution)/shard_map/ppermute | solution.py:48
  73.5 7.8 %collective-permute-start.4 = (f32[64,512]{1,0:T(8,128)S(1)}, f32[64,512]{1,0:T(8,128)S(1)}, u32[]{:S(2)}, u32[]{:S(2)}) collective-permute-start(f32[64,512]{1,0:T(8,128)S(1)} %convolution_subtract_fusion.2), channel_id=1, source_target_pairs={{0,8},{8,16},{16,24},{1,9},{9,17},{17,25},{2,10},{10,18},{18,26},{... | collective-permute-start | bytes 393224 | tf_op jit(solution)/shard_map/ppermute | solution.py:48
  81.9 7.8 %collective-permute-start.5 = (f32[64,512]{1,0:T(8,128)S(1)}, f32[64,512]{1,0:T(8,128)S(1)}, u32[]{:S(2)}, u32[]{:S(2)}) collective-permute-start(f32[64,512]{1,0:T(8,128)S(1)} %convolution_subtract_fusion.1), channel_id=1, source_target_pairs={{0,8},{8,16},{16,24},{1,9},{9,17},{17,25},{2,10},{10,18},{18,26},{... | collective-permute-start | bytes 393224 | tf_op jit(solution)/shard_map/ppermute | solution.py:48
Sparse Core Ops, SparseCore 0:
  8.9 27.2 all-gather.4
  37.9 22.5 all-gather.6

commit v2 on v1

v2 whole, which is shorter than its diff:
```python
import functools

import jax
import jax.numpy as jnp
from jax import lax
from jax.experimental import pallas as pl
from jax.experimental.pallas import tpu as pltpu
from jax.sharding import PartitionSpec as P

MESH = pl.DeviceIdType.MESH
contract_last = (((1,), (1,)), ((), ()))
DEPTH_CHUNKS = 4
CHAIN_CHUNKS = 1


def dot_t(a, b):
    return lax.dot_general(a, b, contract_last, preferred_element_type=jnp.float32)


def halves(x):
    hi = x.astype(jnp.bfloat16)
    return hi, (x - hi.astype(jnp.float32)).astype(jnp.bfloat16)


def dot3(x, w_hi, w_lo):
    hi, lo = halves(x)
    return dot_t(hi, w_hi) + (dot_t(hi, w_lo) + dot_t(lo, w_hi))


def kernel(
    n, n_slab, split_ahead,
    src, leaf, slot, merge, lift, coup, inv, bnd, out,
    sv, lv, mv, ltv, full, split, lift_split, xb, kept, lsend, lrecv,
    bb, pv, st, ob,
    loc, lev_s, lev_r, g_s, g_r, p_s, p_r, ch_s, ch_r, o_s, o_r, b_s, b_r,
):
    me, slab = lax.axis_index("box"), lax.axis_index("slab")
    chips = n // 2
    chip = me // 2
    core = me - 2 * chip
    mate = me + 1 - 2 * core
    rows, points = pv.shape
    width = points // n
    total, edges = lsend.shape
    half0 = total // 2
    depth = lv.shape[1]
    kd = depth // DEPTH_CHUNKS
    levels = n.bit_length() - 1
    shards = (coup, inv)

    def side(level):
        mask = 2 ** (levels - 1 - level)
        bit = lax.rem(me // mask, 2)
        return bit, me + mask - 2 * mask * bit

    bit0, _ = side(0)
    starts = ((1 - bit0) * half0, bit0 * half0)

    local = []

    def read(a, b):
        c = pltpu.make_async_copy(a, b, loc.at[len(local)])
        c.start()
        local.append(c)
        return c

    read_merge = read(merge, mv)
    read_leaf, read_src = [], ([], [])
    for which in range(2):
        for k in range(DEPTH_CHUNKS):
            cols = pl.ds(k * kd, kd)
            if which == 0:
                read_leaf.append(read(leaf.at[:, cols], lv.at[:, cols]))
            at = pl.ds(pl.multiple_of(starts[which], half0), half0)
            read_src[which].append(read(src.at[at, cols], sv.at[which, :, cols]))
    read_lift = read(lift, ltv)

    def shard_at(i, owner):
        return full.at[i, pl.ds(pl.multiple_of(owner * width, width), width), :]

    read_own = [read(shards[i], shard_at(i, me)) for i in range(2)]

    barrier = pltpu.get_barrier_semaphore()
    for d in range(1, n):
        pl.semaphore_signal(
            barrier, inc=1, device_id={"box": lax.rem(me + d, n)}, device_id_type=MESH
        )
    for d in (1, n_slab - 1):
        pl.semaphore_signal(
            barrier, inc=1, device_id={"slab": lax.rem(slab + d, n_slab)}, device_id_type=MESH
        )
    pl.semaphore_wait(barrier, n + 1)

    def remote(a, b, s, r, to, axis="box"):
        return pltpu.make_async_remote_copy(
            src_ref=a, dst_ref=b, send_sem=s, recv_sem=r,
            device_id={axis: to}, device_id_type=MESH,
        )

    def line(direction, t, i):
        step = 1 if direction == 0 else -1
        owner = me - 2 * step * t
        ok_chip = chip - step * t
        to_chip = chip + step
        a = shards[i] if t == 0 else shard_at(i, owner)
        ok = (ok_chip >= 0) & (ok_chip < chips) & (to_chip >= 0) & (to_chip < chips)
        return ok, remote(
            a, shard_at(i, owner), g_s.at[direction, t, i], g_r.at[direction, t, i], me + 2 * step
        )

    def arrival(direction, t, i):
        step = 1 if direction == 0 else -1
        ref = shard_at(i, me - 2 * step * (t + 1))
        return remote(
            ref, ref, g_s.at[direction, t, i], g_r.at[direction, t, i], me - 2 * step
        )

    def came(direction, t):
        owner_chip = chip - (t + 1 if direction == 0 else -t - 1)
        return (owner_chip >= 0) & (owner_chip < chips)

    def share(direction, t, i):
        step = 1 if direction == 0 else -1
        owner = me - 2 * step * (t + 1)
        k = 0 if t < 0 else 1 + 2 * t + direction
        a = shards[i] if t < 0 else shard_at(i, owner)
        return remote(a, shard_at(i, owner), p_s.at[k, i], p_r.at[k, i], mate)

    def shared(direction, t, i):
        step = 1 if direction == 0 else -1
        k = 0 if t < 0 else 1 + 2 * t + direction
        ref = shard_at(i, mate - 2 * step * (t + 1))
        return remote(ref, ref, p_s.at[k, i], p_r.at[k, i], mate)

    def launch(t):
        for direction in range(2):
            for i in range(2):
                ok, copy = line(direction, t, i)
                pl.when(ok)(copy.start)

    def take(t):
        for direction in range(2):
            for i in range(2):
                pl.when(came(direction, t))(arrival(direction, t, i).wait_recv)
        if t + 1 < chips - 1:
            launch(t + 1)
        for direction in range(2):
            for i in range(2):
                pl.when(came(direction, t))(share(direction, t, i).start)

    launch(0)
    for i in range(2):
        share(0, -1, i).start()

    def rows_of(who):
        return pl.ds(pl.multiple_of(who * rows, rows), rows)

    @pl.when(slab == 0)
    def _():
        pltpu.make_async_copy(bnd.at[rows_of(me), :], bb.at[me], b_s.at[0]).start()
        for d in range(1, n):
            to = lax.rem(me + d, n)
            remote(bnd.at[rows_of(to), :], bb.at[me], b_s.at[d], b_r.at[d], to).start()

    read_merge.wait()
    m_hi, m_lo = halves(mv[...])
    place = (
        lax.broadcasted_iota(jnp.int32, (edges, edges), 0) == slot[...]
    ).astype(jnp.float32).astype(jnp.bfloat16)
    first = (dot_t(m_hi, place).astype(jnp.bfloat16), dot_t(m_lo, place).astype(jnp.bfloat16))

    def flux(which):
        acc = None
        for k in range(DEPTH_CHUNKS):
            if which == 0:
                read_leaf[k].wait()
            read_src[which][k].wait()
            cols = slice(k * kd, (k + 1) * kd)
            part = dot_t(sv[which, :, cols], lv[:, cols])
            acc = part if acc is None else acc + part
        return acc

    offset = 0
    sent = []
    for level in range(levels):
        bit, to = side(level)
        half = total >> (level + 1)
        area = pl.ds(offset, half)
        offset += half

        def part_of(which):
            if level == 0:
                return dot3(flux(which), *first)
            at = bit if which == 1 else 1 - bit
            x = xb[pl.ds(pl.multiple_of(at * half, half), half), :]
            return dot3(x, m_hi, m_lo)

        lsend[area, :] = part_of(0)
        copy = remote(lsend.at[area, :], lrecv.at[area, :], lev_s.at[level], lev_r.at[level], to)
        copy.start()
        sent.append(copy)
        kept[pl.ds(0, half), :] = part_of(1)
        if level == 0:
            read_lift.wait()
            lift_split[0], lift_split[1] = halves(ltv[...])
            for c in read_own:
                c.wait()
        if level < chips - 1:
            take(level)
        copy.wait_recv()
        xb[pl.ds(0, half), :] = kept[pl.ds(0, half), :] + lrecv[area, :]

    load = dot3(xb[pl.ds(0, rows), :], lift_split[0], lift_split[1])

    for t in range(levels, chips - 1):
        take(t)
    for i in range(2):
        shared(0, -1, i).wait_recv()
    for t in range(chips - 1):
        for direction in range(2):
            for i in range(2):
                pl.when(came(direction, t))(shared(direction, t, i).wait_recv)

    block = min(points, 256)
    if split_ahead:
        for i in range(2):
            for r in range(0, points, block):
                hi, lo = halves(full[i, r : r + block, :])
                split[2 * i, r : r + block, :] = hi
                split[2 * i + 1, r : r + block, :] = lo

    def times(x, i):
        if split_ahead:
            return dot3(x, split[2 * i], split[2 * i + 1])
        parts = [dot3(x, *halves(full[i, r : r + block, :])) for r in range(0, points, block)]
        return jnp.concatenate(parts, axis=1)

    @pl.when(slab == 0)
    def _():
        pltpu.make_async_copy(bnd.at[rows_of(me), :], bb.at[me], b_s.at[0]).wait()
        for d in range(1, n):
            who = lax.rem(me + n - d, n)
            remote(bb.at[who], bb.at[who], b_s.at[d], b_r.at[d], who).wait_recv()
        for j in range(n):
            pv[:, j * width : (j + 1) * width] = bb[j]

    def hop(c):
        at = pl.ds(c * (rows // CHAIN_CHUNKS), rows // CHAIN_CHUNKS)
        return remote(
            st.at[at, :], pv.at[at, :], ch_s.at[c], ch_r.at[c],
            lax.rem(slab + 1, n_slab), "slab",
        )

    for c in range(CHAIN_CHUNKS):
        lo_row = c * (rows // CHAIN_CHUNKS)
        hi_row = lo_row + rows // CHAIN_CHUNKS
        pl.when(slab > 0)(hop(c).wait_recv)
        corrected = load[lo_row:hi_row] - times(pv[lo_row:hi_row, :], 0)
        state = times(corrected, 1)
        st[lo_row:hi_row, :] = state
        pl.when(slab < n_slab - 1)(hop(c).start)
        for j in range(n):
            ob[j, lo_row:hi_row, :] = state[:, j * width : (j + 1) * width]

    own = pltpu.make_async_copy(ob.at[me], out.at[rows_of(me), :], o_s.at[0])
    own.start()
    outs = []
    for d in range(1, n):
        to = lax.rem(me + d, n)
        copy = remote(ob.at[to], out.at[rows_of(me), :], o_s.at[d], o_r.at[d], to)
        copy.start()
        outs.append(copy)

    for copy in sent:
        copy.wait_send()
    for i in range(2):
        share(0, -1, i).wait_send()
    for t in range(chips - 1):
        for direction in range(2):
            for i in range(2):
                ok, copy = line(direction, t, i)
                pl.when(ok)(copy.wait_send)
                pl.when(came(direction, t))(share(direction, t, i).wait_send)

    @pl.when(slab == 0)
    def _():
        for d in range(1, n):
            to = lax.rem(me + d, n)
            remote(bnd.at[rows_of(to), :], bb.at[me], b_s.at[d], b_r.at[d], to).wait_send()

    for c in range(CHAIN_CHUNKS):
        pl.when(slab < n_slab - 1)(hop(c).wait_send)
    own.wait()
    for d in range(1, n):
        outs[d - 1].wait_send()
        who = lax.rem(me + n - d, n)
        remote(ob.at[who], out.at[rows_of(who), :], o_s.at[d], o_r.at[d], who).wait_recv()


def on_device(sources, leaf_ops, edge_slot, merge_ops, lift_ops, coupling, inverse, boundary):
    n, n_slab = lax.axis_size("box"), lax.axis_size("slab")
    total, depth = sources.shape[2:]
    edges = leaf_ops.shape[2]
    points = lift_ops.shape[2]
    rows, width = total // n, points // n
    chips, levels = n // 2, n.bit_length() - 1
    split_ahead = points * points <= 2**20
    f32, bf16 = jnp.float32, jnp.bfloat16
    hbm = pl.BlockSpec(memory_space=pl.ANY)
    dma = lambda *s: pltpu.SemaphoreType.DMA(s)
    result = pl.pallas_call(
        functools.partial(kernel, n, n_slab, split_ahead),
        out_shape=jax.ShapeDtypeStruct((total, width), f32),
        in_specs=[hbm, hbm, pl.BlockSpec(memory_space=pltpu.VMEM)] + [hbm] * 5,
        out_specs=hbm,
        scratch_shapes=[
            pltpu.VMEM((2, total // 2, depth), bf16),
            pltpu.VMEM((edges, depth), bf16),
            pltpu.VMEM((edges, edges), f32),
            pltpu.VMEM((points, edges), f32),
            pltpu.VMEM((2, points, points), f32),
            pltpu.VMEM((4, points, points) if split_ahead else (4, 16, 128), bf16),
            pltpu.VMEM((2, points, edges), bf16),
            pltpu.VMEM((total // 2, edges), f32),
            pltpu.VMEM((total // 2, edges), f32),
            pltpu.VMEM((total, edges), f32),
            pltpu.VMEM((total, edges), f32),
            pltpu.VMEM((n, rows, width), f32),
            pltpu.VMEM((rows, points), f32),
            pltpu.VMEM((rows, points), f32),
            pltpu.VMEM((n, rows, width), f32),
            dma(3 * DEPTH_CHUNKS + 4),
            dma(levels), dma(levels),
            dma(2, chips - 1, 2), dma(2, chips - 1, 2),
            dma(2 * chips, 2), dma(2 * chips, 2),
            dma(CHAIN_CHUNKS), dma(CHAIN_CHUNKS),
            dma(n), dma(n), dma(n), dma(n),
        ],
        compiler_params=pltpu.CompilerParams(collective_id=0, has_side_effects=True),
        name="slab_solve",
    )(
        sources[0, 0], leaf_ops[0, 0], edge_slot[0], merge_ops[0, 0], lift_ops[0, 0],
        coupling[0], inverse[0], boundary,
    )
    return result[None]


def solution(mesh):
    return jax.shard_map(
        on_device,
        mesh=mesh,
        in_specs=(
            P("slab", "box", None, None),
            P("slab", "box", None, None),
            P("slab", "box", None),
            P("slab", "box", None, None),
            P("slab", "box", None, None),
            P("slab", "box", None),
            P("slab", "box", None),
            P(None, "box"),
        ),
        out_specs=P("slab", None, "box"),
        check_vma=False,
    )
```

time: 110 us -> 71.8 us (0.65)
  the two profiles are of different devices: /device:TPU:4 before, /device:TPU:7 now
where the time goes in v2:
time: 71.8 us; the launch traced here: 71.6 us
  Pallas kernels  68.1 us (95%)
  local copies, waits for them, and re-layouts  3.45 us (5%)
    pallas_call x1, Pallas kernels, on_device(): pl.pallas_call(functools.partial(kernel, n, n_slab, split_ahead), out_sha...  68.1 us
    unnamed x1, local copies, waits for them, and re-layouts  1.73 us
    broadcast_in_dim x1, local copies, waits for them, and re-layouts, on_device(): return result[None]  1.72 us

profile of v2, /device:TPU:7, one launch (start us, length us, event | category | flops | bytes accessed | tf_op | source)
XLA Modules:
  0.0 71.6 jit_solution(2005695280260105600)
XLA Ops:
  0.0 1.7 %copy.9.bnd = f32[512,64]{1,0:T(8,128)} copy(f32[512,64]{0,1:T(8,128)} %param.15) | data formatting | bytes 262144 | tf_op args[7]
  1.7 68.1 %slab_solve.1 = f32[512,64]{1,0:T(8,128)} custom-call(bf16[512,4096]{1,0:T(8,128)(2,1)} %bitcast.8, bf16[256,4096]{1,0:T(8,128)(2,1)} %bitcast.9, s32[1,256]{1,0:T(1,128)} %bitcast.15, f32[256,256]{1,0:T(8,128)} %bitcast.12, f32[512,256]{1,0:T(8,128)} %bitcast.11, f32[64,512]{1,0:T(8,128)} %bitcast.13, f32[64,512]{1,0:T(8,128)} %bitcast.14, f32[512,64]{1,0:T(8,128)} %copy.9.bnd), custom_call_target="tpu_custom_call" | custom-call | tf_op jit(solution)/shard_map/slab_solve/pallas_call | solution.py:311
  69.9 1.7 %copy.10 = f32[1,512,64]{1,2,0:T(8,128)} copy(f32[1,512,64]{2,1,0:T(8,128)} %bitcast.10) | data formatting | bytes 262144 | tf_op jit(solution)/shard_map/broadcast_in_dim | solution.py:345

commit v3 on v2

v3 whole, which is shorter than its diff:
```python
import functools

import jax
import jax.numpy as jnp
from jax import lax
from jax.experimental import pallas as pl
from jax.experimental.pallas import tpu as pltpu
from jax.sharding import PartitionSpec as P

MESH = pl.DeviceIdType.MESH
contract_last = (((1,), (1,)), ((), ()))
DEPTH_CHUNKS = 2
CHAIN_CHUNKS = 2


def dot_t(a, b):
    return lax.dot_general(a, b, contract_last, preferred_element_type=jnp.float32)


def halves(x):
    hi = x.astype(jnp.bfloat16)
    return hi, (x - hi.astype(jnp.float32)).astype(jnp.bfloat16)


def dot3(x, w_hi, w_lo):
    hi, lo = halves(x)
    return dot_t(hi, w_hi) + (dot_t(hi, w_lo) + dot_t(lo, w_hi))


def kernel(
    n, n_slab, split_ahead,
    src, leaf, slot, merge, lift, coup, inv, bnd, out,
    sv, lv, mv, ltv, full, split, lift_split, lsend, lrecv,
    bst, bv, pv, st, cz, ob, rb,
    loc, lev_s, lev_r, g_s, g_r, p_s, p_r, ch_s, ch_r, o_s, o_r, b_s, b_r, x_s, x_r,
):
    me, slab = lax.axis_index("box"), lax.axis_index("slab")
    chips = n // 2
    chip = me // 2
    core = me - 2 * chip
    mate = me + 1 - 2 * core
    rows, points = pv.shape
    width = points // n
    total, edges = lsend.shape
    depth = lv.shape[1]
    kd = depth // DEPTH_CHUNKS
    levels = n.bit_length() - 1
    aid = split_ahead
    helper = n_slab - 1 if aid else 0
    is_helper = slab == helper
    coup0 = 2 if aid else 0

    def peer(level):
        mask = 2 ** (levels - 1 - level)
        return me + mask - 2 * mask * lax.rem(me // mask, 2)

    def block_of(position):
        block = 0
        for q in range(levels):
            bit = lax.rem(me // 2**q, 2)
            block = block + 2**q * (bit if (position >> q) & 1 else 1 - bit)
        return block

    local = []

    def read(a, b):
        c = pltpu.make_async_copy(a, b, loc.at[len(local)])
        c.start()
        local.append(c)
        return c

    def rows_of(who):
        return pl.ds(pl.multiple_of(who * rows, rows), rows)

    read_merge = read(merge, mv)
    read_leaf, read_src = [], ([], [])
    for which in range(2):
        for k in range(DEPTH_CHUNKS):
            cols = pl.ds(k * kd, kd)
            if which == 0:
                read_leaf.append(read(leaf.at[:, cols], lv.at[:, cols]))
            read_src[which].append([
                read(src.at[rows_of(block_of(p)), cols], sv.at[pl.ds(p * rows, rows), cols])
                for p in range(which * n // 2, (which + 1) * n // 2)
            ])
    read_lift = read(lift, ltv)

    def shard_at(i, owner):
        return full.at[i, pl.ds(pl.multiple_of(owner * width, width), width), :]

    read_own = [read(m, shard_at(i, me)) for i, m in enumerate((coup, inv))]

    barrier = pltpu.get_barrier_semaphore()
    for d in range(1, n):
        pl.semaphore_signal(
            barrier, inc=1, device_id={"box": lax.rem(me + d, n)}, device_id_type=MESH
        )
    for d in (1, n_slab - 1):
        pl.semaphore_signal(
            barrier, inc=1, device_id={"slab": lax.rem(slab + d, n_slab)}, device_id_type=MESH
        )
    pl.semaphore_wait(barrier, n + 1)

    def remote(a, b, s, r, to, axis="box"):
        return pltpu.make_async_remote_copy(
            src_ref=a, dst_ref=b, send_sem=s, recv_sem=r,
            device_id={axis: to}, device_id_type=MESH,
        )

    def line(direction, t, i):
        step = 1 if direction == 0 else -1
        owner = me - 2 * step * t
        ok_chip = chip - step * t
        to_chip = chip + step
        a = (coup, inv)[i] if t == 0 and i < 2 else shard_at(i, owner)
        ok = (ok_chip >= 0) & (ok_chip < chips) & (to_chip >= 0) & (to_chip < chips)
        return ok, remote(
            a, shard_at(i, owner), g_s.at[direction, t, i], g_r.at[direction, t, i], me + 2 * step
        )

    def arrival(direction, t, i):
        step = 1 if direction == 0 else -1
        ref = shard_at(i, me - 2 * step * (t + 1))
        return remote(
            ref, ref, g_s.at[direction, t, i], g_r.at[direction, t, i], me - 2 * step
        )

    def came(direction, t):
        owner_chip = chip - (t + 1 if direction == 0 else -t - 1)
        return (owner_chip >= 0) & (owner_chip < chips)

    def share(direction, t, i):
        step = 1 if direction == 0 else -1
        owner = me - 2 * step * (t + 1)
        k = 0 if t < 0 else 1 + 2 * t + direction
        a = (coup, inv)[i] if t < 0 and i < 2 else shard_at(i, owner)
        return remote(a, shard_at(i, owner), p_s.at[k, i], p_r.at[k, i], mate)

    def shared(direction, t, i):
        step = 1 if direction == 0 else -1
        k = 0 if t < 0 else 1 + 2 * t + direction
        ref = shard_at(i, mate - 2 * step * (t + 1))
        return remote(ref, ref, p_s.at[k, i], p_r.at[k, i], mate)

    def launch(t, i):
        if t == 0:
            share(0, -1, i).start()
        for direction in range(2):
            ok, copy = line(direction, t, i)
            pl.when(ok)(copy.start)

    def take(t, i):
        for direction in range(2):
            pl.when(came(direction, t))(arrival(direction, t, i).wait_recv)
        if t + 1 < chips - 1:
            launch(t + 1, i)
        for direction in range(2):
            pl.when(came(direction, t))(share(direction, t, i).start)

    def all_here(i):
        shared(0, -1, i).wait_recv()
        for t in range(chips - 1):
            for direction in range(2):
                pl.when(came(direction, t))(shared(direction, t, i).wait_recv)

    def all_sent(i):
        share(0, -1, i).wait_send()
        for t in range(chips - 1):
            for direction in range(2):
                ok, copy = line(direction, t, i)
                pl.when(ok)(copy.wait_send)
                pl.when(came(direction, t))(share(direction, t, i).wait_send)

    def coupled(f, *args):
        if aid:
            pl.when(slab != 0)(lambda: f(*args))
        else:
            f(*args)

    def lend():
        return remote(coup, shard_at(2, me), x_s.at[0], x_r.at[0], helper, "slab")

    def answer():
        return remote(st, pv, x_s.at[1], x_r.at[1], 0, "slab")

    def edge_block(d):
        to = lax.rem(me + d, n)
        at = pl.ds(pl.multiple_of(me * width, width), width)
        return remote(bst.at[to], bv.at[at, :], b_s.at[d], b_r.at[d], to)

    own_edge = pltpu.make_async_copy(
        bst.at[me], bv.at[pl.ds(pl.multiple_of(me * width, width), width), :], b_s.at[0]
    )

    if aid:
        pl.when(slab == 0)(lend().start)

    @pl.when(is_helper)
    def _():
        for j in range(n):
            bst[j] = bnd[:, j * rows : (j + 1) * rows]
        own_edge.start()
        for d in range(1, n):
            edge_block(d).start()
        if aid:
            lend().wait_recv()
            launch(0, 2)

    launch(0, 1)
    coupled(launch, 0, 0)

    read_merge.wait()
    m_hi, m_lo = halves(mv[...])
    place = (
        lax.broadcasted_iota(jnp.int32, (edges, edges), 0) == slot[...]
    ).astype(jnp.float32).astype(jnp.bfloat16)
    first = (dot_t(m_hi, place).astype(jnp.bfloat16), dot_t(m_lo, place).astype(jnp.bfloat16))

    def flux(which):
        acc = None
        for k in range(DEPTH_CHUNKS):
            if which == 0:
                read_leaf[k].wait()
            for c in read_src[which][k]:
                c.wait()
            cols = slice(k * kd, (k + 1) * kd)
            part = dot_t(sv[which * total // 2 : (which + 1) * total // 2, cols], lv[:, cols])
            acc = part if acc is None else acc + part
        return acc

    offset = 0
    sent = []
    place_of = []
    for level in range(levels):
        half = total >> (level + 1)
        pieces = 2 if level < levels - 1 else 1
        place_of.append((offset, half // pieces, pieces))
        offset += half

    def give(level, y):
        start, size, pieces = place_of[level]
        lsend[start : start + size * pieces, :] = y
        copies = []
        for c in range(pieces):
            at = pl.ds(start + c * size, size)
            copy = remote(
                lsend.at[at, :], lrecv.at[at, :], lev_s.at[level, c], lev_r.at[level, c], peer(level)
            )
            copy.start()
            copies.append(copy)
        sent.extend(copies)
        return copies

    def got(level, c):
        start, size, _ = place_of[level]
        return lrecv[start + c * size : start + (c + 1) * size, :]

    copies = give(0, dot3(flux(0), *first))
    keep = dot3(flux(1), *first)
    read_lift.wait()
    lift_split[0], lift_split[1] = halves(ltv[...])
    for c in read_own:
        c.wait()

    if aid:
        @pl.when(is_helper)
        def _():
            for t in range(chips - 1):
                take(t, 2)
            all_here(2)
            own_edge.wait()
            for d in range(1, n):
                edge_block(d).wait_recv()
            st[...] = dot3(bv[...].T, *halves(full[2]))
            answer().start()

    taken = 0
    for level in range(levels):
        size = place_of[level][1]
        if taken < chips - 1:
            take(taken, 1)
            coupled(take, taken, 0)
            taken += 1
        copies[0].wait_recv()
        x = keep[:size] + got(level, 0)
        if level < levels - 1:
            later = give(level + 1, dot3(x, m_hi, m_lo))
            copies[1].wait_recv()
            keep = dot3(keep[size:] + got(level, 1), m_hi, m_lo)
            copies = later
    load = dot3(x, lift_split[0], lift_split[1])

    for t in range(taken, chips - 1):
        take(t, 1)
        coupled(take, t, 0)

    block = min(points, 256)

    def prepare(i):
        if split_ahead:
            for r in range(0, points, block):
                hi, lo = halves(full[i, r : r + block, :])
                split[2 * i, r : r + block, :] = hi
                split[2 * i + 1, r : r + block, :] = lo

    all_here(1)
    prepare(1)

    def ready():
        all_here(0)
        prepare(0)

    coupled(ready)

    def rows_at(i, r):
        if split_ahead:
            return split[2 * i, r : r + block, :], split[2 * i + 1, r : r + block, :]
        return halves(full[i, r : r + block, :])

    def times(x, i):
        if split_ahead:
            return dot3(x, split[2 * i], split[2 * i + 1])
        return jnp.concatenate(
            [dot3(x, *rows_at(i, r)) for r in range(0, points, block)], axis=1
        )

    if not aid:
        @pl.when(is_helper)
        def _():
            own_edge.wait()
            for d in range(1, n):
                edge_block(d).wait_recv()
            pv[...] = bv[...].T

    size = rows // CHAIN_CHUNKS

    def hop(c):
        at = pl.ds(c * size, size)
        return remote(
            st.at[at, :], pv.at[at, :], ch_s.at[c], ch_r.at[c],
            lax.rem(slab + 1, n_slab), "slab",
        )

    if aid:
        pl.when(slab == 0)(answer().wait_recv)
    for c in range(CHAIN_CHUNKS):
        at = slice(c * size, (c + 1) * size)
        mine = load[at]

        def later_slab():
            cz[at, :] = mine - times(pv[at, :], 0)

        def first_slab():
            cz[at, :] = mine - pv[at, :]

        pl.when(slab > 0)(hop(c).wait_recv)
        if aid:
            pl.when(slab > 0)(later_slab)
            pl.when(slab == 0)(first_slab)
        else:
            later_slab()

        @pl.when(slab < n_slab - 1)
        def _():
            st[at, :] = times(cz[at, :], 1)
            hop(c).start()

    c_hi, c_lo = halves(cz[...])
    for r in range(0, points, block):
        w_hi, w_lo = rows_at(1, r)
        turned = dot_t(w_hi, c_hi) + (dot_t(w_hi, c_lo) + dot_t(w_lo, c_hi))
        for j in range(block // width):
            ob[r // width + j] = turned[j * width : (j + 1) * width]

    own = pltpu.make_async_copy(ob.at[me], rb.at[me], o_s.at[0])
    own.start()
    outs = []
    for d in range(1, n):
        to = lax.rem(me + d, n)
        copy = remote(ob.at[to], rb.at[me], o_s.at[d], o_r.at[d], to)
        copy.start()
        outs.append(copy)

    for copy in sent:
        copy.wait_send()
    all_sent(1)
    coupled(all_sent, 0)

    @pl.when(is_helper)
    def _():
        for d in range(1, n):
            edge_block(d).wait_send()
        if aid:
            all_sent(2)
            answer().wait_send()

    if aid:
        pl.when(slab == 0)(lend().wait_send)
    for c in range(CHAIN_CHUNKS):
        pl.when(slab < n_slab - 1)(hop(c).wait_send)
    own.wait()
    for d in range(1, n):
        who = lax.rem(me + n - d, n)
        remote(ob.at[who], rb.at[who], o_s.at[d], o_r.at[d], who).wait_recv()
    for j in range(n):
        out[:, j * rows : (j + 1) * rows] = rb[j]
    for copy in outs:
        copy.wait_send()


def on_device(sources, leaf_ops, edge_slot, merge_ops, lift_ops, coupling, inverse, boundary):
    n, n_slab = lax.axis_size("box"), lax.axis_size("slab")
    total, depth = sources.shape[2:]
    edges = leaf_ops.shape[2]
    points = lift_ops.shape[2]
    rows, width = total // n, points // n
    chips, levels = n // 2, n.bit_length() - 1
    split_ahead = points * points <= 2**20
    f32, bf16 = jnp.float32, jnp.bfloat16
    hbm = pl.BlockSpec(memory_space=pl.ANY)
    dma = lambda *s: pltpu.SemaphoreType.DMA(s)
    vmem = pl.BlockSpec(memory_space=pltpu.VMEM)
    result = pl.pallas_call(
        functools.partial(kernel, n, n_slab, split_ahead),
        out_shape=jax.ShapeDtypeStruct((width, total), f32),
        in_specs=[hbm, hbm, vmem] + [hbm] * 4 + [vmem],
        out_specs=vmem,
        scratch_shapes=[
            pltpu.VMEM((total, depth), bf16),
            pltpu.VMEM((edges, depth), bf16),
            pltpu.VMEM((edges, edges), f32),
            pltpu.VMEM((points, edges), f32),
            pltpu.VMEM((3 if split_ahead else 2, points, points), f32),
            pltpu.VMEM((4, points, points) if split_ahead else (4, 16, 128), bf16),
            pltpu.VMEM((2, points, edges), bf16),
            pltpu.VMEM((total, edges), f32),
            pltpu.VMEM((total, edges), f32),
            pltpu.VMEM((n, width, rows), f32),
            pltpu.VMEM((points, rows), f32),
            pltpu.VMEM((rows, points), f32),
            pltpu.VMEM((rows, points), f32),
            pltpu.VMEM((rows, points), f32),
            pltpu.VMEM((n, width, rows), f32),
            pltpu.VMEM((n, width, rows), f32),
            dma(DEPTH_CHUNKS * (n + 1) + 4),
            dma(levels, 2), dma(levels, 2),
            dma(2, chips - 1, 3), dma(2, chips - 1, 3),
            dma(2 * chips, 3), dma(2 * chips, 3),
            dma(CHAIN_CHUNKS), dma(CHAIN_CHUNKS),
            dma(n), dma(n), dma(n), dma(n), dma(2), dma(2),
        ],
        compiler_params=pltpu.CompilerParams(collective_id=0, has_side_effects=True),
        name="slab_solve",
    )(
        sources[0, 0], leaf_ops[0, 0], edge_slot[0], merge_ops[0, 0], lift_ops[0, 0],
        coupling[0], inverse[0], boundary.T,
    )
    return result.T[None]


def solution(mesh):
    return jax.shard_map(
        on_device,
        mesh=mesh,
        in_specs=(
            P("slab", "box", None, None),
            P("slab", "box", None, None),
            P("slab", "box", None),
            P("slab", "box", None, None),
            P("slab", "box", None, None),
            P("slab", "box", None),
            P("slab", "box", None),
            P(None, "box"),
        ),
        out_specs=P("slab", None, "box"),
        check_vma=False,
    )
```

time: 71.8 us -> 70.4 us (0.981)
  local copies, waits for them, and re-layouts: 3.45 us -> 1.57 us
    broadcast_in_dim x1 -> x0, local copies, waits for them, and re-layouts: 1.72 us -> none  [on_device(): return result[None]]
where the time goes in v3:
time: 70.4 us; the launch traced here: 70.2 us
  Pallas kernels  68.7 us (98%)
  local copies, waits for them, and re-layouts  1.57 us (2%)
    pallas_call x1, Pallas kernels, on_device(): pl.pallas_call(functools.partial(kernel, n, n_slab, split_ahead), out_sha...  68.7 us
    unnamed x1, local copies, waits for them, and re-layouts  1.57 us

profile of v3, /device:TPU:7, one launch (start us, length us, event | category | flops | bytes accessed | tf_op | source)
XLA Modules:
  0.0 70.2 jit_solution(9997816177559245691)
XLA Ops:
  0.0 68.7 %slab_solve.1 = f32[64,512]{1,0:T(8,128)} custom-call(bf16[512,4096]{1,0:T(8,128)(2,1)} %bitcast.11, bf16[256,4096]{1,0:T(8,128)(2,1)} %bitcast.12, s32[1,256]{1,0:T(1,128)} %bitcast.19, f32[256,256]{1,0:T(8,128)} %bitcast.15, f32[512,256]{1,0:T(8,128)} %bitcast.14, f32[64,512]{1,0:T(8,128)} %bitcast.16, f32[64,512]{1,0:T(8,128)} %bitcast.17, f32[64,512]{1,0:T(8,128)} %bitcast.18), custom_call_target="tpu_custom_call" | custom-call | tf_op jit(solution)/shard_map/slab_solve/pallas_call | solution.py:423
  68.7 1.6 %copy.10 = f32[1,512,64]{1,2,0:T(8,128)} copy(f32[1,512,64]{1,2,0:T(8,128)} %bitcast.13) | data formatting | bytes 262144

commit v4 on v3

--- a/solution.py
+++ b/solution.py
@@ -10,7 +10,7 @@
 MESH = pl.DeviceIdType.MESH
 contract_last = (((1,), (1,)), ((), ()))
 DEPTH_CHUNKS = 2
-CHAIN_CHUNKS = 2
+CHAIN_CHUNKS = 4
 
 
 def dot_t(a, b):
@@ -45,7 +45,7 @@
     depth = lv.shape[1]
     kd = depth // DEPTH_CHUNKS
     levels = n.bit_length() - 1
-    aid = split_ahead
+    aid = False
     helper = n_slab - 1 if aid else 0
     is_helper = slab == helper
     coup0 = 2 if aid else 0
@@ -332,7 +332,8 @@
                 edge_block(d).wait_recv()
             pv[...] = bv[...].T
 
-    size = rows // CHAIN_CHUNKS
+    chunks = max(1, min(CHAIN_CHUNKS, rows // 16))
+    size = rows // chunks
 
     def hop(c):
         at = pl.ds(c * size, size)
@@ -343,7 +344,7 @@
 
     if aid:
         pl.when(slab == 0)(answer().wait_recv)
-    for c in range(CHAIN_CHUNKS):
+    for c in range(chunks):
         at = slice(c * size, (c + 1) * size)
         mine = load[at]
 
@@ -396,7 +397,7 @@
 
     if aid:
         pl.when(slab == 0)(lend().wait_send)
-    for c in range(CHAIN_CHUNKS):
+    for c in range(chunks):
         pl.when(slab < n_slab - 1)(hop(c).wait_send)
     own.wait()
     for d in range(1, n):
@@ -430,7 +431,7 @@
             pltpu.VMEM((edges, depth), bf16),
             pltpu.VMEM((edges, edges), f32),
             pltpu.VMEM((points, edges), f32),
-            pltpu.VMEM((3 if split_ahead else 2, points, points), f32),
+            pltpu.VMEM((2, points, points), f32),
             pltpu.VMEM((4, points, points) if split_ahead else (4, 16, 128), bf16),
             pltpu.VMEM((2, points, edges), bf16),
             pltpu.VMEM((total, edges), f32),

time: 70.4 us -> 63.7 us (0.905)
  Pallas kernels: 68.7 us -> 61.6 us
    pallas_call x1, Pallas kernels: 68.7 us -> 61.6 us  [on_device(): pl.pallas_call(functools.partial(kernel, n, n_slab, split_ahead), out_sha...]
where the time goes in v4:
time: 63.7 us; the launch traced here: 63.2 us
  Pallas kernels  61.6 us (97%)
  local copies, waits for them, and re-layouts  1.57 us (2%)
    pallas_call x1, Pallas kernels, on_device(): pl.pallas_call(functools.partial(kernel, n, n_slab, split_ahead), out_sha...  61.6 us
    unnamed x1, local copies, waits for them, and re-layouts  1.57 us

profile of v4, /device:TPU:7, one launch (start us, length us, event | category | flops | bytes accessed | tf_op | source)
XLA Modules:
  0.0 63.2 jit_solution(8361170852877040886)
XLA Ops:
  0.0 61.6 %slab_solve.1 = f32[64,512]{1,0:T(8,128)} custom-call(bf16[512,4096]{1,0:T(8,128)(2,1)} %bitcast.11, bf16[256,4096]{1,0:T(8,128)(2,1)} %bitcast.12, s32[1,256]{1,0:T(1,128)} %bitcast.19, f32[256,256]{1,0:T(8,128)} %bitcast.15, f32[512,256]{1,0:T(8,128)} %bitcast.14, f32[64,512]{1,0:T(8,128)} %bitcast.16, f32[64,512]{1,0:T(8,128)} %bitcast.17, f32[64,512]{1,0:T(8,128)} %bitcast.18), custom_call_target="tpu_custom_call" | custom-call | tf_op jit(solution)/shard_map/slab_solve/pallas_call | solution.py:424
  61.6 1.6 %copy.10 = f32[1,512,64]{1,2,0:T(8,128)} copy(f32[1,512,64]{1,2,0:T(8,128)} %bitcast.13) | data formatting | bytes 262144
